TPU v7x, 32 devices: a whole 2x2x4 slice. The times are simulated.
32 devices in a mesh: row: 2 (over x), col: 16 (over z, y, core).
Axes of the slice: x: 2, y: 2, z: 4, core: 2. Of those that a mesh axis runs over, the one named last changes fastest.
Arguments:
- pair_state: bfloat16 [256, 256, 256], P('row', 'col'), may hold values from -6 to 6
- residue_mask: int32 [256], replicated, may hold values 0 or 1
- chain_ids: int32 [256], replicated, may hold values from 0 to 3, never falling along the last dimension, each value on 1 to 128 neighbouring positions
- gain_transition: float32 [256], replicated, may hold values from 0.1 to 1.9
- hidden_weight: bfloat16 [256, 1024], replicated, may hold values from -0.375 to 0.375
- out_weight: bfloat16 [1024, 256], replicated, may hold values from -0.1875 to 0.1875
- gain_attention: float32 [256], replicated, may hold values from 0.1 to 1.9
- query_weight: bfloat16 [256, 256], replicated, may hold values from -4 to 4
- key_weight: bfloat16 [256, 256], replicated, may hold values from -4 to 4
- value_weight: bfloat16 [256, 256], replicated, may hold values from -0.375 to 0.375
- gate_weight: bfloat16 [256, 256], replicated, may hold values from -0.375 to 0.375
- bias_weight: bfloat16 [256, 8], replicated, may hold values from -0.375 to 0.375
- chain_weight: float32 [8], replicated, may hold values from -2 to 2
- output_weight: bfloat16 [256, 256], replicated, may hold values from -4 to 4
Outputs:
- symmetric_pair: bfloat16 [256, 256, 256], P('row', 'col')
All inputs are finite; a program needn't handle non-finite values.
Results may differ from a plain program's by a relative error of at most 0.004.
The roundings to bfloat16 on the way count: a program that leaves them out, or rounds other values in their place, can miss the bound.
Values may be sent and summed in bfloat16 or wider, within the bound.
A program may use at most 128 MiB of HBM per device.

v0:
```python
import functools
import math

import jax
import jax.numpy as jnp
from jax import lax
from jax.experimental import pallas as pl
from jax.experimental.pallas import tpu as pltpu
from jax.sharding import PartitionSpec as P

MESH = pl.DeviceIdType.MESH
VMEM_LIMIT = 60 * 1024 * 1024
LOG2_E = math.log2(math.e)

mask_penalty = 1000000000.0
norm_epsilon = 1e-05


def normalize(values, gain):
    center = values - jnp.mean(values, axis=-1, keepdims=True)
    variance = jnp.mean(center * center, axis=-1, keepdims=True)
    return center * lax.rsqrt(variance + norm_epsilon) * gain


def mirror(tile):
    tile_rows, tile_cols, channels = tile.shape
    col_count = lax.axis_size("col")
    row_count = lax.axis_size("row")
    col_ratio = col_count // row_count
    piece_len = tile_cols * tile_cols // col_count
    sectioned = tile.reshape(col_ratio, col_count, piece_len, channels)
    sectioned = lax.all_to_all(sectioned, "col", split_axis=1, concat_axis=1, tiled=True)
    sectioned = sectioned.reshape(col_ratio, row_count, col_ratio, piece_len, channels)
    sectioned = lax.all_to_all(sectioned, "row", split_axis=1, concat_axis=1, tiled=True)
    sectioned = jnp.transpose(sectioned, (1, 0, 2, 3, 4)).reshape(
        col_count, col_ratio, piece_len, channels
    )
    sectioned = lax.all_to_all(sectioned, "col", split_axis=0, concat_axis=0, tiled=True)
    sectioned = jnp.transpose(sectioned, (1, 0, 2, 3)).reshape(
        col_ratio, tile_cols, tile_cols, channels
    )
    return jnp.transpose(sectioned, (0, 2, 1, 3)).reshape(tile_rows, tile_cols, channels)


def attend(query_part, gate_part, key_part, value_part, bias_part, head_count, output_weight):
    query_total = query_part.shape[0]
    key_total = key_part.shape[0]
    head_dim = query_part.shape[1] // head_count
    score_scale = 1.0 / math.sqrt(head_dim)
    query_heads = query_part.reshape(query_total, head_count, head_dim)
    key_heads = key_part.reshape(key_total, head_count, head_dim)
    value_heads = value_part.reshape(key_total, head_count, head_dim)
    scores = (
        jnp.einsum("jhd,khd->hjk", query_heads, key_heads, preferred_element_type=jnp.float32)
        * score_scale
        + bias_part
    )
    row_max = jnp.max(scores, axis=-1, keepdims=True)
    exponent = jnp.exp(scores - row_max)
    attn_weights = (exponent / jnp.sum(exponent, axis=-1, keepdims=True)).astype(jnp.bfloat16)
    mixture = jnp.einsum(
        "hjk,khd->jhd", attn_weights, value_heads, preferred_element_type=jnp.float32
    )
    gated = (gate_part * mixture.reshape(query_total, head_count * head_dim)).astype(jnp.bfloat16)
    return jnp.dot(gated, output_weight, preferred_element_type=jnp.float32).astype(jnp.bfloat16)


def mirror_layout(
    normed_tile,
    bias_tile,
    chain_ids,
    penalty,
    chain_weight,
    query_weight,
    key_weight,
    value_weight,
    gate_weight,
    output_weight,
):
    tile_rows, tile_cols, channels = normed_tile.shape
    head_count = bias_tile.shape[0]
    row_start = lax.axis_index("row") * tile_rows
    flat_tile = normed_tile.reshape(tile_rows * tile_cols, channels)
    key_tile = (
        jnp.dot(flat_tile, key_weight, preferred_element_type=jnp.float32)
        .astype(jnp.bfloat16)
        .reshape(tile_rows, tile_cols, -1)
    )
    value_tile = (
        jnp.dot(flat_tile, value_weight, preferred_element_type=jnp.float32)
        .astype(jnp.bfloat16)
        .reshape(tile_rows, tile_cols, -1)
    )
    key_all, value_all = (
        lax.all_gather(key_tile, "row", axis=0, tiled=True),
        lax.all_gather(value_tile, "row", axis=0, tiled=True),
    )
    bias_rows = lax.all_gather(bias_tile, "col", axis=2, tiled=True)
    chain_rows = lax.dynamic_slice_in_dim(chain_ids, row_start, tile_rows, 0)
    same_chain = (chain_rows[:, None] == chain_ids[None, :]).astype(jnp.float32)
    bias_full = (
        bias_rows.astype(jnp.float32)
        + chain_weight[:, None, None] * same_chain[None]
        - penalty[None, None, :]
    )
    query_tile = (
        jnp.dot(flat_tile, query_weight, preferred_element_type=jnp.float32)
        .astype(jnp.bfloat16)
        .reshape(tile_rows, tile_cols, -1)
    )
    gate_tile = jax.nn.sigmoid(
        jnp.dot(flat_tile, gate_weight, preferred_element_type=jnp.float32)
    ).reshape(tile_rows, tile_cols, -1)

    def one_column(position):
        query_part = lax.dynamic_index_in_dim(query_tile, position, 1, keepdims=False)
        gate_part = lax.dynamic_index_in_dim(gate_tile, position, 1, keepdims=False)
        key_part = lax.dynamic_index_in_dim(key_all, position, 1, keepdims=False)
        value_part = lax.dynamic_index_in_dim(value_all, position, 1, keepdims=False)
        return attend(
            query_part, gate_part, key_part, value_part, bias_full, head_count, output_weight
        )

    results = lax.map(one_column, jnp.arange(tile_cols, dtype=jnp.int32))
    return jnp.transpose(results, (1, 0, 2))


def tile_layout(
    pair_state,
    residue_mask,
    chain_ids,
    gain_transition,
    hidden_weight,
    out_weight,
    gain_attention,
    query_weight,
    key_weight,
    value_weight,
    gate_weight,
    bias_weight,
    chain_weight,
    output_weight,
):
    tile_rows, tile_cols, channels = pair_state.shape
    head_count = chain_weight.shape[0]
    mirrored = mirror(pair_state)
    sym_tile = pair_state.astype(jnp.float32) + mirrored.astype(jnp.float32)
    flat_sym = sym_tile.reshape(tile_rows * tile_cols, channels)
    first_norm = normalize(flat_sym, gain_transition).astype(jnp.bfloat16)
    hidden_act = jax.nn.relu(
        jnp.dot(first_norm, hidden_weight, preferred_element_type=jnp.float32)
    ).astype(jnp.bfloat16)
    carried = flat_sym + jnp.dot(hidden_act, out_weight, preferred_element_type=jnp.float32)
    normed = normalize(carried, gain_attention).astype(jnp.bfloat16)
    bias_tile = (
        jnp.einsum("pd,dh->hp", normed, bias_weight, preferred_element_type=jnp.float32)
        .astype(jnp.bfloat16)
        .reshape(head_count, tile_rows, tile_cols)
    )
    penalty = mask_penalty * (1 - residue_mask).astype(jnp.float32)
    normed_tile = normed.reshape(tile_rows, tile_cols, channels)
    arguments = (
        normed_tile,
        bias_tile,
        chain_ids,
        penalty,
        chain_weight,
        query_weight,
        key_weight,
        value_weight,
        gate_weight,
        output_weight,
    )
    own_update = mirror_layout(*arguments)
    other_update = mirror(own_update)
    total = (
        2.0 * carried.reshape(tile_rows, tile_cols, channels)
        + own_update.astype(jnp.float32)
        + other_update.astype(jnp.float32)
    )
    return total.astype(jnp.bfloat16)


def greet_all(row_count, col_count):
    device_total = row_count * col_count
    me = lax.axis_index("col") * row_count + lax.axis_index("row")
    barrier = pltpu.get_barrier_semaphore()

    def greet(step, carry):
        peer = lax.rem(me + step, device_total)
        pl.semaphore_signal(
            barrier,
            inc=1,
            device_id=(lax.rem(peer, row_count), peer // row_count),
            device_id_type=MESH,
        )
        return carry

    lax.fori_loop(1, device_total, greet, 0)
    pl.semaphore_wait(barrier, device_total - 1)


def transition_kernel(
    row_count,
    col_count,
    tile_ref,
    turned_ref,
    gain_transition_ref,
    hidden_weight_ref,
    out_weight_ref,
    gain_attention_ref,
    bias_weight_ref,
    carried_ref,
    normed_ref,
    bias_ref,
    row_buf,
    col_buf,
    relay_buf,
    relay_send,
    relay_recv,
    row_send,
    row_recv,
    col_send,
    col_recv,
    bias_send,
    bias_recv,
    pair_send,
    pair_recv,
):
    tile_rows, tile_cols, channels = tile_ref.shape
    own = tile_cols // row_count
    half = own // 2
    span = col_count // row_count
    chip_total = row_count * col_count // 2
    row_id, col_id = lax.axis_index("row"), lax.axis_index("col")
    me = col_id * row_count + row_id
    side = lax.rem(col_id, 2)
    chip = (col_id // 2) * row_count + row_id
    greet_all(row_count, col_count)

    def relay_copy(other, slot, part):
        return pltpu.make_async_remote_copy(
            src_ref=tile_ref.at[pl.ds((slot * row_count + other) * own + part * half, half)],
            dst_ref=relay_buf.at[row_id, slot, part],
            send_sem=relay_send.at[other, slot, part],
            recv_sem=relay_recv.at[row_id, slot, part],
            device_id=(other, col_id),
            device_id_type=MESH,
        )

    def start_rows(origin, slot, part, source):
        target = origin * span + slot
        columns = pl.ds(pl.multiple_of(col_id * tile_cols, tile_cols), tile_cols)
        landing = row_buf.at[pl.ds(part * half, half), columns, :]

        @pl.when(target != col_id)
        def _():
            pltpu.make_async_remote_copy(
                src_ref=source,
                dst_ref=landing,
                send_sem=row_send.at[origin, slot, part],
                recv_sem=row_recv.at[col_id, part],
                device_id=(row_id, target),
                device_id_type=MESH,
            ).start()

        @pl.when(target == col_id)
        def _():
            pltpu.make_async_copy(source, landing, row_recv.at[col_id, part]).start()

    def col_remote(other, part):
        return pltpu.make_async_remote_copy(
            src_ref=turned_ref.at[pl.ds(other * own + part * half, half)],
            dst_ref=col_buf.at[
                pl.ds(part * half, half), pl.ds(pl.multiple_of(row_id * tile_rows, tile_rows), tile_rows), :
            ],
            send_sem=col_send.at[other, part],
            recv_sem=col_recv.at[row_id, part],
            device_id=(other, col_id),
            device_id_type=MESH,
        )

    def over_rows(body):
        def one(step, carry):
            body(lax.rem(row_id + step, row_count))
            return carry

        lax.fori_loop(1, row_count, one, 0)

    def over_slots(body):
        def one(step, carry):
            body(lax.rem(col_id + step, span))
            return carry

        lax.fori_loop(0, span, one, 0)

    own_columns = pl.ds(pl.multiple_of(row_id * tile_rows, tile_rows), tile_rows)

    def own_col(part):
        return pltpu.make_async_copy(
            turned_ref.at[pl.ds(row_id * own + part * half, half)],
            col_buf.at[pl.ds(part * half, half), own_columns, :],
            col_recv.at[row_id, part],
        )

    def direct(slot, part):
        first = (slot * row_count + row_id) * own + part * half
        start_rows(row_id, slot, part, tile_ref.at[pl.ds(first, half)])

    def pass_on(origin, slot, part):
        arrived = relay_buf.at[origin, slot, part]
        pltpu.make_async_copy(arrived, arrived, relay_recv.at[origin, slot, part]).wait()
        start_rows(origin, slot, part, arrived)

    for part in range(2):
        over_rows(lambda other: over_slots(lambda slot: relay_copy(other, slot, part).start()))
    for part in range(2):
        over_slots(lambda slot: direct(slot, part))
        over_rows(lambda other: col_remote(other, part).start())
        own_col(part).start()
    for part in range(2):
        over_rows(lambda origin: over_slots(lambda slot: pass_on(origin, slot, part)))

    def wait_part(part):
        def wait_row(other, carry):
            columns = pl.ds(pl.multiple_of(other * tile_cols, tile_cols), tile_cols)
            landed = row_buf.at[pl.ds(part * half, half), columns, :]
            pltpu.make_async_copy(landed, landed, row_recv.at[other, part]).wait()
            return carry

        lax.fori_loop(0, col_count, wait_row, 0)

        def wait_col(other, carry):
            columns = pl.ds(pl.multiple_of(other * tile_rows, tile_rows), tile_rows)
            landed = col_buf.at[pl.ds(part * half, half), columns, :]
            pltpu.make_async_copy(landed, landed, col_recv.at[other, part]).wait()
            return carry

        lax.fori_loop(0, row_count, wait_col, 0)

    def over_chips(body):
        def one(step, carry):
            body(lax.rem(chip + step, chip_total))
            return carry

        lax.fori_loop(1, chip_total, one, 0)

    def chip_place(other, which):
        return lax.rem(other, row_count), (other // row_count) * 2 + which

    def slab(other, which):
        place = chip_place(other, which)
        return bias_ref.at[pl.ds((place[1] * row_count + place[0]) * own, own)]

    def one_row(position, carry):
        sym_row = row_buf[position].astype(jnp.float32) + col_buf[position].astype(jnp.float32)
        first_norm = normalize(sym_row, gain_transition_ref[...]).astype(jnp.bfloat16)
        hidden_act = jax.nn.relu(
            jnp.dot(first_norm, hidden_weight_ref[...], preferred_element_type=jnp.float32)
        ).astype(jnp.bfloat16)
        carried = sym_row + jnp.dot(
            hidden_act, out_weight_ref[...], preferred_element_type=jnp.float32
        )
        carried_ref[position] = carried
        normed = normalize(carried, gain_attention_ref[...]).astype(jnp.bfloat16)
        normed_ref[position] = normed
        bias_ref[me * own + position] = lax.dot_general(
            bias_weight_ref[...],
            normed,
            (((1,), (1,)), ((), ())),
            preferred_element_type=jnp.float32,
        ).astype(jnp.bfloat16)
        over_chips(
            lambda other: pltpu.make_async_remote_copy(
                src_ref=bias_ref.at[me * own + position],
                dst_ref=bias_ref.at[me * own + position],
                send_sem=bias_send.at[other],
                recv_sem=bias_recv.at[chip],
                device_id=chip_place(other, side),
                device_id_type=MESH,
            ).start()
        )
        return carry

    def part_rows(part, carry):
        wait_part(part)
        lax.fori_loop(part * half, (part + 1) * half, one_row, 0)
        return carry

    lax.fori_loop(0, 2, part_rows, 0)

    def to_pair(other):
        return pltpu.make_async_remote_copy(
            src_ref=slab(other, side),
            dst_ref=slab(other, side),
            send_sem=pair_send.at[other],
            recv_sem=pair_recv.at[other],
            device_id=(row_id, col_id + 1 - 2 * side),
            device_id_type=MESH,
        )

    to_pair(chip).start()

    def hand_over(other):
        landed = slab(other, side)
        pltpu.make_async_copy(landed, landed, bias_recv.at[other]).wait()
        to_pair(other).start()

    over_chips(hand_over)

    def close_pair(other, carry):
        landed = slab(other, 1 - side)
        pltpu.make_async_copy(landed, landed, pair_recv.at[other]).wait()
        to_pair(other).wait_send()
        return carry

    lax.fori_loop(0, chip_total, close_pair, 0)

    def close_chip(other):
        sent = slab(chip, side)
        pltpu.make_async_copy(sent, sent, bias_send.at[other]).wait()

    over_chips(close_chip)

    def close_rows(origin, slot, part):
        @pl.when(origin * span + slot != col_id)
        def _():
            sent = relay_buf.at[origin, slot, part]
            pltpu.make_async_copy(sent, sent, row_send.at[origin, slot, part]).wait()

    for part in range(2):
        over_slots(lambda slot: close_rows(row_id, slot, part))
        over_rows(lambda origin: over_slots(lambda slot: close_rows(origin, slot, part)))
        over_rows(lambda other: over_slots(lambda slot: relay_copy(other, slot, part).wait_send()))
        over_rows(lambda other: col_remote(other, part).wait_send())


def attention_kernel(
    row_count,
    col_count,
    carried_ref,
    normed_ref,
    bias_ref,
    query_weight_ref,
    key_weight_ref,
    value_weight_ref,
    gate_weight_ref,
    output_weight_ref,
    out_ref,
    total,
    update_buf,
    recv_buf,
    turned,
    sum_buf,
    score_buf,
    weight_buf,
    query_turned,
    value_turned,
    gate_turned,
    update_send,
    update_recv,
    sum_send,
    sum_recv,
):
    own, length, channels = normed_ref.shape
    head_count = bias_ref.shape[0]
    inner_total = key_weight_ref.shape[1]
    head_dim = inner_total // head_count
    score_scale = LOG2_E / math.sqrt(head_dim)
    device_total = row_count * col_count
    row_id, col_id = lax.axis_index("row"), lax.axis_index("col")
    me = col_id * row_count + row_id
    query_turned[...] = query_weight_ref[...].T
    value_turned[...] = value_weight_ref[...].T
    gate_turned[...] = gate_weight_ref[...].T
    greet_all(row_count, col_count)

    def over_peers(body):
        def one(step, carry):
            body(lax.rem(me + step, device_total))
            return carry

        lax.fori_loop(1, device_total, one, 0)

    def over_rows(body):
        def one(step, carry):
            body(lax.rem(row_id + step, row_count))
            return carry

        lax.fori_loop(1, row_count, one, 0)

    strip = min(128, length)
    band = min(inner_total, max(128, head_dim))
    heads_in_band = band // head_dim
    head_of_lane = lax.broadcasted_iota(jnp.int32, (1, band), 1) // head_dim

    def one_row(position, carry):
        normed = normed_ref[position]
        normed_turned = normed.T

        def project(weight_ref):
            return jnp.dot(weight_ref[...], normed_turned, preferred_element_type=jnp.float32)

        keys = jnp.dot(
            normed, key_weight_ref[...], preferred_element_type=jnp.float32
        ).astype(jnp.bfloat16)
        queries = project(query_turned).astype(jnp.bfloat16)
        values = project(value_turned).astype(jnp.bfloat16)
        gates = jax.nn.sigmoid(project(gate_turned))
        def score(head):
            first = head // heads_in_band * band
            chosen = (head_of_lane == head % heads_in_band).astype(jnp.bfloat16)
            score_buf[head] = (
                jnp.dot(
                    keys[:, first : first + band] * chosen,
                    queries[first : first + band],
                    preferred_element_type=jnp.float32,
                )
                * score_scale
                + bias_ref[head]
            )

        mixed = []
        for head in range(4):
            score(head)
        for head in range(head_count):
            if head + 4 < head_count:
                score(head + 4)
            rows = slice(head * head_dim, (head + 1) * head_dim)
            for start in range(0, length, strip):
                places = slice(start, start + strip)
                scores = score_buf[head, :, places]
                exponent = jnp.exp2(scores - jnp.max(scores, axis=0, keepdims=True))
                weight_buf[head, :, places] = (
                    exponent * (1.0 / jnp.sum(exponent, axis=0, keepdims=True))
                ).astype(jnp.bfloat16)
            mixture = jnp.dot(values[rows], weight_buf[head], preferred_element_type=jnp.float32)
            mixed.append((gates[rows] * mixture).astype(jnp.bfloat16))
        gated = jnp.concatenate(mixed, axis=0).T
        update = jnp.dot(gated, output_weight_ref[...], preferred_element_type=jnp.float32)
        update = update.reshape(device_total, own, channels).astype(jnp.bfloat16)
        update_buf[position] = update
        recv_buf[me, position] = update_buf[position, me]
        total[position] = 2.0 * carried_ref[position] + update.astype(jnp.float32).reshape(
            length, channels
        )
        over_peers(
            lambda peer: pltpu.make_async_remote_copy(
                src_ref=update_buf.at[position, peer],
                dst_ref=recv_buf.at[me, position],
                send_sem=update_send.at[peer],
                recv_sem=update_recv.at[position, me],
                device_id=(lax.rem(peer, row_count), peer // row_count),
                device_id_type=MESH,
            ).start()
        )
        return carry

    lax.fori_loop(0, own, one_row, 0)
    for position in range(own):
        turned[:, :, position, :] = total[position].reshape(device_total, own, channels)

    def summed(other, position):
        devices = pl.ds(other * col_count, col_count)
        return (
            turned[devices, position] + recv_buf[devices, position].astype(jnp.float32)
        ).astype(jnp.bfloat16)

    def sum_remote(other, position):
        return pltpu.make_async_remote_copy(
            src_ref=sum_buf.at[other, :, position],
            dst_ref=out_ref.at[row_id, :, position],
            send_sem=sum_send.at[other, position],
            recv_sem=sum_recv.at[row_id, position],
            device_id=(other, col_id),
            device_id_type=MESH,
        )

    def finish_position(position, carry):
        def arrived(peer):
            landed = recv_buf.at[peer, position]
            pltpu.make_async_copy(landed, landed, update_recv.at[position, peer]).wait()

        over_peers(arrived)

        def pass_sum(other):
            sum_buf[other, :, position] = summed(other, position)
            sum_remote(other, position).start()

        over_rows(pass_sum)
        out_ref[row_id, :, position] = summed(row_id, position)
        return carry

    lax.fori_loop(0, own, finish_position, 0)

    def close_peer(peer):
        sent = recv_buf.at[peer]
        pltpu.make_async_copy(sent, sent, update_send.at[peer]).wait()

    over_peers(close_peer)

    def close_position(position, carry):
        def close_row(other):
            landed = out_ref.at[other, :, position]
            pltpu.make_async_copy(landed, landed, sum_recv.at[other, position]).wait()
            sum_remote(other, position).wait_send()

        over_rows(close_row)
        return carry

    lax.fori_loop(0, own, close_position, 0)


def owned_columns(
    pair_state,
    residue_mask,
    chain_ids,
    gain_transition,
    hidden_weight,
    out_weight,
    gain_attention,
    query_weight,
    key_weight,
    value_weight,
    gate_weight,
    bias_weight,
    chain_weight,
    output_weight,
):
    tile_rows, tile_cols, channels = pair_state.shape
    row_count, col_count = lax.axis_size("row"), lax.axis_size("col")
    device_total = row_count * col_count
    head_count = chain_weight.shape[0]
    length = tile_rows * row_count
    own = tile_cols // row_count
    span = col_count // row_count
    in_vmem = pl.BlockSpec(memory_space=pltpu.VMEM)
    dma = pltpu.SemaphoreType.DMA
    carried, normed, bias_rows = pl.pallas_call(
        functools.partial(transition_kernel, row_count, col_count),
        out_shape=(
            jax.ShapeDtypeStruct((own, length, channels), jnp.float32),
            jax.ShapeDtypeStruct((own, length, channels), jnp.bfloat16),
            jax.ShapeDtypeStruct((length, head_count, length), jnp.bfloat16),
        ),
        in_specs=[in_vmem] * 7,
        out_specs=(in_vmem,) * 3,
        scratch_shapes=[
            pltpu.VMEM((own, length, channels), jnp.bfloat16),
            pltpu.VMEM((own, length, channels), jnp.bfloat16),
            pltpu.VMEM((row_count, span, 2, own // 2, tile_cols, channels), jnp.bfloat16),
            dma((row_count, span, 2)),
            dma((row_count, span, 2)),
            dma((row_count, span, 2)),
            dma((col_count, 2)),
            dma((row_count, 2)),
            dma((row_count, 2)),
            dma((device_total // 2,)),
            dma((device_total // 2,)),
            dma((device_total // 2,)),
            dma((device_total // 2,)),
        ],
        compiler_params=pltpu.CompilerParams(
            collective_id=0, has_side_effects=True, vmem_limit_bytes=VMEM_LIMIT
        ),
        name="transition",
    )(
        pair_state,
        jnp.transpose(pair_state, (1, 0, 2)),
        gain_transition[None, :],
        hidden_weight,
        out_weight,
        gain_attention[None, :],
        bias_weight.T,
    )
    penalty = mask_penalty * (1 - residue_mask).astype(jnp.float32)
    same_chain = (chain_ids[:, None] == chain_ids[None, :]).astype(jnp.float32)
    bias_full = (
        jnp.transpose(bias_rows, (1, 0, 2)).astype(jnp.float32)
        + chain_weight[:, None, None] * same_chain[None]
        - penalty[None, :, None]
    ) * LOG2_E
    pieces = pl.pallas_call(
        functools.partial(attention_kernel, row_count, col_count),
        out_shape=jax.ShapeDtypeStruct((row_count, col_count, own, own, channels), jnp.bfloat16),
        in_specs=[in_vmem] * 8,
        out_specs=in_vmem,
        scratch_shapes=[
            pltpu.VMEM((own, length, channels), jnp.float32),
            pltpu.VMEM((own, device_total, own, channels), jnp.bfloat16),
            pltpu.VMEM((device_total, own, own, channels), jnp.bfloat16),
            pltpu.VMEM((device_total, own, own, channels), jnp.float32),
            pltpu.VMEM((row_count, col_count, own, own, channels), jnp.bfloat16),
            pltpu.VMEM((head_count, length, length), jnp.float32),
            pltpu.VMEM((head_count, length, length), jnp.bfloat16),
            pltpu.VMEM(query_weight.shape[::-1], jnp.bfloat16),
            pltpu.VMEM(value_weight.shape[::-1], jnp.bfloat16),
            pltpu.VMEM(gate_weight.shape[::-1], jnp.bfloat16),
            dma((device_total,)),
            dma((own, device_total)),
            dma((row_count, own)),
            dma((row_count, own)),
        ],
        compiler_params=pltpu.CompilerParams(
            collective_id=1, has_side_effects=True, vmem_limit_bytes=VMEM_LIMIT
        ),
        name="attention",
    )(
        carried,
        normed,
        bias_full,
        query_weight,
        key_weight,
        value_weight,
        gate_weight,
        output_weight,
    )
    pieces = pieces.reshape(row_count, tile_rows, own, channels)
    return jnp.transpose(pieces, (1, 0, 2, 3)).reshape(tile_rows, tile_cols, channels)


def per_device(pair_state, *others):
    tile_cols = pair_state.shape[1]
    row_count, col_count = lax.axis_size("row"), lax.axis_size("col")
    own = tile_cols // row_count
    if own % 8 == 0 and col_count % 2 == 0 and col_count % row_count == 0:
        return owned_columns(pair_state, *others)
    return tile_layout(pair_state, *others)


def solution(mesh):
    placed = (
        P("row", "col", None),
        P(),
        P(),
        P(),
        P(),
        P(),
        P(),
        P(),
        P(),
        P(),
        P(),
        P(),
        P(),
        P(),
    )
    return jax.shard_map(
        per_device, mesh=mesh, in_specs=placed, out_specs=P("row", "col", None), check_vma=False
    )
```

profile of v0, /device:TPU:0, one launch (start us, length us, event | category | flops | bytes accessed | tf_op | source)
XLA Modules:
  0.0 109.0 jit_solution(13457429841198464822)
XLA Ops:
  0.0 0.7 convert_multiply_fusion
  0.7 0.9 compare_convert_fusion
  1.5 2.5 %copy.22 = bf16[128,16,256]{2,0,1:T(8,128)(2,1)} copy(bf16[128,16,256]{2,1,0:T(8,128)(2,1)} %tile_ref.1) | data formatting | bytes 2097152 | tf_op args[0]
  4.1 0.0 copy-start
  4.1 55.5 %transition.1 = (f32[8,256,256]{2,1,0:T(8,128)}, bf16[8,256,256]{2,1,0:T(8,128)(2,1)}, bf16[256,8,256]{2,1,0:T(8,128)(2,1)}) custom-call(bf16[128,16,256]{2,1,0:T(8,128)(2,1)} %tile_ref.1, bf16[16,128,256]{2,1,0:T(8,128)(2,1)} %bitcast.18, f32[1,256]{1,0:T(1,128)} %bitcast.21, bf16[256,1024]{1,0:T(8,128)(2,1)} %hidden_weight_ref.1, ...), custom_call_target="tpu_custom_call" | custom-call | tf_op jit(solution)/shard_map/transition/pallas_call | solution.py:639
  59.6 0.0 copy-done
  59.6 2.9 %fusion.1.bias_ref = f32[8,256,256]{2,1,0:T(8,128)} fusion(bf16[256,8,256]{2,1,0:T(8,128)(2,1)} %get-tuple-element.10, f32[256]{0:T(256)S(1)} %convert_multiply_fusion, f32[256,256]{1,0:T(8,128)S(1)} %compare_convert_fusion, f32[8]{0:T(128)S(1)} %copy-done), kind=kLoop, calls=%fused_computation.2 | loop fusion | flops 2621440 | bytes 3408928 | tf_op jit(solution)/shard_map/mul | solution.py:678
  62.5 44.2 %attention.1 = bf16[2,16,8,8,256]{4,3,2,1,0:T(8,128)(2,1)} custom-call(f32[8,256,256]{2,1,0:T(8,128)} %get-tuple-element.8.carried_ref, bf16[8,256,256]{2,1,0:T(8,128)(2,1)} %get-tuple-element.9.normed_ref, f32[8,256,256]{2,1,0:T(8,128)} %fusion.1.bias_ref, bf16[256,256]{1,0:T(8,128)(2,1)} %query_weight_ref.1, bf16[256,256]{1,0:T(8,128)(2,1)} %key_weight_ref.1, ...), custom_call_target="tpu_custom_call" | custom-call | tf_op jit(solution)/shard_map/attention/pallas_call | solution.py:683
  106.7 2.3 %copy.21 = bf16[128,2,8,256]{3,2,1,0:T(8,128)(2,1)} copy(bf16[128,2,8,256]{3,2,0,1:T(8,128)(2,1)} %bitcast.19) | data formatting | bytes 2097152 | tf_op jit(solution)/shard_map/transpose | solution.py:719
Async XLA Ops:
  4.1 55.5 %copy-start = (f32[8]{0:T(128)S(1)}, f32[8]{0:T(128)}, u32[]{:S(2)}) copy-start(f32[8]{0:T(128)} %param.26) | copy-start | bytes 100
where the time goes:
time: 109 us
  Pallas kernels  99.7 us (91%)
  local copies, waits for them, and re-layouts  4.81 us (4%)
  other arithmetic  4.43 us (4%)
    pallas_call x1, Pallas kernels, owned_columns(): pl.pallas_call(functools.partial(transition_kernel, row_count, col_count)...  55.5 us
    pallas_call x1, Pallas kernels, owned_columns(): pl.pallas_call(functools.partial(attention_kernel, row_count, col_count),...  44.2 us
    mul x1, other arithmetic, owned_columns(): (jnp.transpose(bias_rows, (1, 0, 2)).astype(jnp.float32) + chain_weight[:...  2.9 us
    unnamed x3, local copies, waits for them, and re-layouts  2.54 us
    transpose x1, local copies, waits for them, and re-layouts, owned_columns(): jnp.transpose(pieces, (1, 0, 2, 3)).reshape(tile_rows, tile_cols, channels)  2.28 us

commit v1 on v0

v1 whole, which is shorter than its diff:
```python
import functools
import math

import jax
import jax.numpy as jnp
from jax import lax
from jax.experimental import pallas as pl
from jax.experimental.pallas import tpu as pltpu
from jax.sharding import PartitionSpec as P

MESH = pl.DeviceIdType.MESH
VMEM_LIMIT = 60 * 1024 * 1024
LOG2_E = math.log2(math.e)
PARTS = 4
LANES = 128

mask_penalty = 1000000000.0
norm_epsilon = 1e-05


def normalize(values, gain):
    center = values - jnp.mean(values, axis=-1, keepdims=True)
    variance = jnp.mean(center * center, axis=-1, keepdims=True)
    return center * lax.rsqrt(variance + norm_epsilon) * gain


def mirror(tile):
    tile_rows, tile_cols, channels = tile.shape
    col_count = lax.axis_size("col")
    row_count = lax.axis_size("row")
    col_ratio = col_count // row_count
    piece_len = tile_cols * tile_cols // col_count
    sectioned = tile.reshape(col_ratio, col_count, piece_len, channels)
    sectioned = lax.all_to_all(sectioned, "col", split_axis=1, concat_axis=1, tiled=True)
    sectioned = sectioned.reshape(col_ratio, row_count, col_ratio, piece_len, channels)
    sectioned = lax.all_to_all(sectioned, "row", split_axis=1, concat_axis=1, tiled=True)
    sectioned = jnp.transpose(sectioned, (1, 0, 2, 3, 4)).reshape(
        col_count, col_ratio, piece_len, channels
    )
    sectioned = lax.all_to_all(sectioned, "col", split_axis=0, concat_axis=0, tiled=True)
    sectioned = jnp.transpose(sectioned, (1, 0, 2, 3)).reshape(
        col_ratio, tile_cols, tile_cols, channels
    )
    return jnp.transpose(sectioned, (0, 2, 1, 3)).reshape(tile_rows, tile_cols, channels)


def attend(query_part, gate_part, key_part, value_part, bias_part, head_count, output_weight):
    query_total = query_part.shape[0]
    key_total = key_part.shape[0]
    head_dim = query_part.shape[1] // head_count
    score_scale = 1.0 / math.sqrt(head_dim)
    query_heads = query_part.reshape(query_total, head_count, head_dim)
    key_heads = key_part.reshape(key_total, head_count, head_dim)
    value_heads = value_part.reshape(key_total, head_count, head_dim)
    scores = (
        jnp.einsum("jhd,khd->hjk", query_heads, key_heads, preferred_element_type=jnp.float32)
        * score_scale
        + bias_part
    )
    row_max = jnp.max(scores, axis=-1, keepdims=True)
    exponent = jnp.exp(scores - row_max)
    attn_weights = (exponent / jnp.sum(exponent, axis=-1, keepdims=True)).astype(jnp.bfloat16)
    mixture = jnp.einsum(
        "hjk,khd->jhd", attn_weights, value_heads, preferred_element_type=jnp.float32
    )
    gated = (gate_part * mixture.reshape(query_total, head_count * head_dim)).astype(jnp.bfloat16)
    return jnp.dot(gated, output_weight, preferred_element_type=jnp.float32).astype(jnp.bfloat16)


def mirror_layout(
    normed_tile,
    bias_tile,
    chain_ids,
    penalty,
    chain_weight,
    query_weight,
    key_weight,
    value_weight,
    gate_weight,
    output_weight,
):
    tile_rows, tile_cols, channels = normed_tile.shape
    head_count = bias_tile.shape[0]
    row_start = lax.axis_index("row") * tile_rows
    flat_tile = normed_tile.reshape(tile_rows * tile_cols, channels)
    key_tile = (
        jnp.dot(flat_tile, key_weight, preferred_element_type=jnp.float32)
        .astype(jnp.bfloat16)
        .reshape(tile_rows, tile_cols, -1)
    )
    value_tile = (
        jnp.dot(flat_tile, value_weight, preferred_element_type=jnp.float32)
        .astype(jnp.bfloat16)
        .reshape(tile_rows, tile_cols, -1)
    )
    key_all, value_all = (
        lax.all_gather(key_tile, "row", axis=0, tiled=True),
        lax.all_gather(value_tile, "row", axis=0, tiled=True),
    )
    bias_rows = lax.all_gather(bias_tile, "col", axis=2, tiled=True)
    chain_rows = lax.dynamic_slice_in_dim(chain_ids, row_start, tile_rows, 0)
    same_chain = (chain_rows[:, None] == chain_ids[None, :]).astype(jnp.float32)
    bias_full = (
        bias_rows.astype(jnp.float32)
        + chain_weight[:, None, None] * same_chain[None]
        - penalty[None, None, :]
    )
    query_tile = (
        jnp.dot(flat_tile, query_weight, preferred_element_type=jnp.float32)
        .astype(jnp.bfloat16)
        .reshape(tile_rows, tile_cols, -1)
    )
    gate_tile = jax.nn.sigmoid(
        jnp.dot(flat_tile, gate_weight, preferred_element_type=jnp.float32)
    ).reshape(tile_rows, tile_cols, -1)

    def one_column(position):
        query_part = lax.dynamic_index_in_dim(query_tile, position, 1, keepdims=False)
        gate_part = lax.dynamic_index_in_dim(gate_tile, position, 1, keepdims=False)
        key_part = lax.dynamic_index_in_dim(key_all, position, 1, keepdims=False)
        value_part = lax.dynamic_index_in_dim(value_all, position, 1, keepdims=False)
        return attend(
            query_part, gate_part, key_part, value_part, bias_full, head_count, output_weight
        )

    results = lax.map(one_column, jnp.arange(tile_cols, dtype=jnp.int32))
    return jnp.transpose(results, (1, 0, 2))


def tile_layout(
    pair_state,
    residue_mask,
    chain_ids,
    gain_transition,
    hidden_weight,
    out_weight,
    gain_attention,
    query_weight,
    key_weight,
    value_weight,
    gate_weight,
    bias_weight,
    chain_weight,
    output_weight,
):
    tile_rows, tile_cols, channels = pair_state.shape
    head_count = chain_weight.shape[0]
    mirrored = mirror(pair_state)
    sym_tile = pair_state.astype(jnp.float32) + mirrored.astype(jnp.float32)
    flat_sym = sym_tile.reshape(tile_rows * tile_cols, channels)
    first_norm = normalize(flat_sym, gain_transition).astype(jnp.bfloat16)
    hidden_act = jax.nn.relu(
        jnp.dot(first_norm, hidden_weight, preferred_element_type=jnp.float32)
    ).astype(jnp.bfloat16)
    carried = flat_sym + jnp.dot(hidden_act, out_weight, preferred_element_type=jnp.float32)
    normed = normalize(carried, gain_attention).astype(jnp.bfloat16)
    bias_tile = (
        jnp.einsum("pd,dh->hp", normed, bias_weight, preferred_element_type=jnp.float32)
        .astype(jnp.bfloat16)
        .reshape(head_count, tile_rows, tile_cols)
    )
    penalty = mask_penalty * (1 - residue_mask).astype(jnp.float32)
    normed_tile = normed.reshape(tile_rows, tile_cols, channels)
    arguments = (
        normed_tile,
        bias_tile,
        chain_ids,
        penalty,
        chain_weight,
        query_weight,
        key_weight,
        value_weight,
        gate_weight,
        output_weight,
    )
    own_update = mirror_layout(*arguments)
    other_update = mirror(own_update)
    total = (
        2.0 * carried.reshape(tile_rows, tile_cols, channels)
        + own_update.astype(jnp.float32)
        + other_update.astype(jnp.float32)
    )
    return total.astype(jnp.bfloat16)


def greet_all(row_count, col_count):
    device_total = row_count * col_count
    me = lax.axis_index("col") * row_count + lax.axis_index("row")
    barrier = pltpu.get_barrier_semaphore()

    def greet(step, carry):
        peer = lax.rem(me + step, device_total)
        pl.semaphore_signal(
            barrier,
            inc=1,
            device_id=(lax.rem(peer, row_count), peer // row_count),
            device_id_type=MESH,
        )
        return carry

    lax.fori_loop(1, device_total, greet, 0)
    pl.semaphore_wait(barrier, device_total - 1)


def layer_kernel(
    row_count,
    col_count,
    tile_ref,
    turned_ref,
    mask_ref,
    chain_ref,
    gain_transition_ref,
    hidden_weight_ref,
    out_weight_ref,
    gain_attention_ref,
    query_weight_ref,
    key_weight_ref,
    value_weight_ref,
    gate_weight_ref,
    bias_weight_ref,
    chain_weight_ref,
    output_weight_ref,
    out_ref,
    row_buf,
    col_buf,
    relay_buf,
    bias_buf,
    same_buf,
    penalty_buf,
    bias_full,
    carried_buf,
    normed_buf,
    key_buf,
    query_buf,
    value_buf,
    gate_buf,
    query_turned,
    value_turned,
    gate_turned,
    score_buf,
    weight_buf,
    update_buf,
    recv_buf,
    turned,
    sum_buf,
    relay_send,
    relay_recv,
    row_send,
    row_recv,
    col_send,
    col_recv,
    bias_send,
    bias_recv,
    pair_send,
    pair_recv,
    update_send,
    update_recv,
    sum_send,
    sum_recv,
):
    span, _, own, tile_cols, channels = tile_ref.shape
    parts, _, rows_in_part = relay_buf.shape[:3]
    length = row_buf.shape[1]
    tile_rows = length // row_count
    head_count = bias_weight_ref.shape[0]
    inner_total = key_weight_ref.shape[1]
    head_dim = inner_total // head_count
    score_scale = LOG2_E / math.sqrt(head_dim)
    device_total = row_count * col_count
    chip_total = device_total // 2
    row_id, col_id = lax.axis_index("row"), lax.axis_index("col")
    other_row = 1 - row_id
    me = col_id * row_count + row_id
    side = lax.rem(col_id, 2)
    pair = col_id // 2
    chip = pair * row_count + row_id
    lane_blocks = [slice(start, start + LANES) for start in range(0, channels, LANES)]

    def loop(first, last, body):
        def one(step, carry):
            body(step)
            return carry

        lax.fori_loop(first, last, one, 0)

    def await_bytes(like, semaphore):
        pltpu.make_async_copy(like, like, semaphore).wait()

    def rows_of(part):
        return pl.ds(part * rows_in_part, rows_in_part)

    def relay_copy(part):
        return pltpu.make_async_remote_copy(
            src_ref=tile_ref.at[:, other_row, rows_of(part)],
            dst_ref=relay_buf.at[part],
            send_sem=relay_send.at[part],
            recv_sem=relay_recv.at[part],
            device_id=(other_row, col_id),
            device_id_type=MESH,
        )

    def start_rows(origin, slot, part, source):
        target = origin * span + slot
        columns = pl.ds(pl.multiple_of(col_id * tile_cols, tile_cols), tile_cols)
        landing = row_buf.at[rows_of(part), columns, :]

        @pl.when(target != col_id)
        def _():
            pltpu.make_async_remote_copy(
                src_ref=source,
                dst_ref=landing,
                send_sem=row_send,
                recv_sem=row_recv.at[part],
                device_id=(row_id, target),
                device_id_type=MESH,
            ).start()

        @pl.when(target == col_id)
        def _():
            pltpu.make_async_copy(source, landing, row_recv.at[part]).start()

    def over_slots(body):
        loop(0, span, lambda step: body(lax.rem(col_id + step, span)))

    def direct(part):
        over_slots(
            lambda slot: start_rows(row_id, slot, part, tile_ref.at[slot, row_id, rows_of(part)])
        )

    def pass_on(part):
        await_bytes(relay_buf.at[part], relay_recv.at[part])
        over_slots(lambda slot: start_rows(other_row, slot, part, relay_buf.at[part, slot]))

    own_columns = pl.ds(pl.multiple_of(row_id * tile_rows, tile_rows), tile_rows)

    def col_remote(part):
        return pltpu.make_async_remote_copy(
            src_ref=turned_ref.at[pl.ds(other_row * own + part * rows_in_part, rows_in_part)],
            dst_ref=col_buf.at[rows_of(part), own_columns, :],
            send_sem=col_send.at[part],
            recv_sem=col_recv.at[part],
            device_id=(other_row, col_id),
            device_id_type=MESH,
        )

    def own_col(part):
        return pltpu.make_async_copy(
            turned_ref.at[pl.ds(row_id * own + part * rows_in_part, rows_in_part)],
            col_buf.at[rows_of(part), own_columns, :],
            col_recv.at[part],
        )

    greet_all(row_count, col_count)

    ahead = min(2, parts)
    for part in range(ahead):
        relay_copy(part).start()
    for part in range(ahead):
        direct(part)
    for part in range(parts):
        col_remote(part).start()
        if part + ahead < parts:
            relay_copy(part + ahead).start()
        own_col(part).start()

    query_turned[...] = query_weight_ref[...].T
    value_turned[...] = value_weight_ref[...].T
    gate_turned[...] = gate_weight_ref[...].T
    chain_row = jnp.broadcast_to(chain_ref[...].astype(jnp.float32), (length, length))
    same_buf[...] = (chain_row.T == chain_row).astype(jnp.float32)
    penalty_row = mask_penalty * (1 - mask_ref[...]).astype(jnp.float32)
    penalty_buf[...] = jnp.broadcast_to(penalty_row, (length, length)).T

    for part in range(ahead):
        pass_on(part)
        if part + ahead < parts:
            direct(part + ahead)

    def bias_piece(part):
        return bias_buf.at[pair, side, row_id, part]

    def send_bias(part):
        def to_chip(step):
            other = lax.rem(chip + step, chip_total)
            pltpu.make_async_remote_copy(
                src_ref=bias_piece(part),
                dst_ref=bias_piece(part),
                send_sem=bias_send,
                recv_sem=bias_recv.at[part],
                device_id=(lax.rem(other, row_count), (other // row_count) * 2 + side),
                device_id_type=MESH,
            ).start()

        loop(1, chip_total, to_chip)

    def to_pair(part):
        return pltpu.make_async_remote_copy(
            src_ref=bias_buf.at[:, side, :, part],
            dst_ref=bias_buf.at[:, side, :, part],
            send_sem=pair_send.at[part],
            recv_sem=pair_recv.at[part],
            device_id=(row_id, col_id + 1 - 2 * side),
            device_id_type=MESH,
        )

    def hand_over(part):
        await_bytes(recv_buf.at[pl.ds(0, chip_total - 1), pl.ds(0, rows_in_part)], bias_recv.at[part])
        to_pair(part).start()

    def transition_row(position):
        sym_row = row_buf[position].astype(jnp.float32) + col_buf[position].astype(jnp.float32)
        first_norm = normalize(sym_row, gain_transition_ref[...]).astype(jnp.bfloat16)
        hidden_act = jax.nn.relu(
            jnp.dot(first_norm, hidden_weight_ref[...], preferred_element_type=jnp.float32)
        ).astype(jnp.bfloat16)
        carried = sym_row + jnp.dot(
            hidden_act, out_weight_ref[...], preferred_element_type=jnp.float32
        )
        carried_buf[position] = carried
        normed = normalize(carried, gain_attention_ref[...]).astype(jnp.bfloat16)
        normed_buf[position] = normed
        part = position // rows_in_part
        bias_buf[pair, side, row_id, part, position - part * rows_in_part] = lax.dot_general(
            bias_weight_ref[...],
            normed,
            (((1,), (1,)), ((), ())),
            preferred_element_type=jnp.float32,
        ).astype(jnp.bfloat16)

    def project_row(position):
        normed = normed_buf[position]
        normed_turned = normed.T

        def project(weight_ref):
            return jnp.dot(weight_ref[...], normed_turned, preferred_element_type=jnp.float32)

        key_buf[position] = jnp.dot(
            normed, key_weight_ref[...], preferred_element_type=jnp.float32
        ).astype(jnp.bfloat16)
        query_buf[position] = project(query_turned).astype(jnp.bfloat16)
        value_buf[position] = project(value_turned).astype(jnp.bfloat16)
        gate_buf[position] = jax.nn.sigmoid(project(gate_turned))

    def one_part(part):
        await_bytes(row_buf.at[rows_of(part)], row_recv.at[part])
        await_bytes(col_buf.at[rows_of(part)], col_recv.at[part])
        loop(part * rows_in_part, (part + 1) * rows_in_part, transition_row)
        send_bias(part)

        @pl.when(part + ahead < parts)
        def _():
            pass_on(part + ahead)

        loop(part * rows_in_part, (part + 1) * rows_in_part, project_row)

        @pl.when(part > 0)
        def _():
            hand_over(part - 1)

    loop(0, parts, one_part)
    hand_over(parts - 1)
    loop(0, parts, lambda part: await_bytes(bias_buf.at[:, side, :, part], pair_recv.at[part]))

    bias_rows = bias_buf.reshape(length * head_count, length)
    for lane, lanes in enumerate(lane_blocks):
        turned[lane] = bias_rows[:, lanes].astype(jnp.float32)
    for head in range(head_count):
        for lane, lanes in enumerate(lane_blocks):
            bias_full[head, :, lanes] = (
                turned[lane, pl.ds(head, length, stride=head_count), :]
                + chain_weight_ref[head] * same_buf[:, lanes]
                - penalty_buf[:, lanes]
            ) * LOG2_E

    strip = min(128, length)
    band = min(inner_total, max(128, head_dim))
    heads_in_band = band // head_dim
    head_of_lane = lax.broadcasted_iota(jnp.int32, (1, band), 1) // head_dim

    def attend_row(position):
        keys, queries, values = key_buf[position], query_buf[position], value_buf[position]

        def score(head):
            first = head // heads_in_band * band
            chosen = (head_of_lane == head % heads_in_band).astype(jnp.bfloat16)
            score_buf[head] = (
                jnp.dot(
                    keys[:, first : first + band] * chosen,
                    queries[first : first + band],
                    preferred_element_type=jnp.float32,
                )
                * score_scale
                + bias_full[head]
            )

        mixed = []
        for head in range(4):
            score(head)
        for head in range(head_count):
            if head + 4 < head_count:
                score(head + 4)
            rows = slice(head * head_dim, (head + 1) * head_dim)
            for start in range(0, length, strip):
                places = slice(start, start + strip)
                scores = score_buf[head, :, places]
                exponent = jnp.exp2(scores - jnp.max(scores, axis=0, keepdims=True))
                weight_buf[head, :, places] = (
                    exponent * (1.0 / jnp.sum(exponent, axis=0, keepdims=True))
                ).astype(jnp.bfloat16)
            mixture = jnp.dot(values[rows], weight_buf[head], preferred_element_type=jnp.float32)
            mixed.append((gate_buf[position, rows] * mixture).astype(jnp.bfloat16))
        gated = jnp.concatenate(mixed, axis=0).T
        update = jnp.dot(gated, output_weight_ref[...], preferred_element_type=jnp.float32)
        update = update.astype(jnp.bfloat16)
        update_buf[position] = update.reshape(device_total, own, channels)
        recv_buf[me, position] = update_buf[position, me]

        def to_peer(step):
            peer = lax.rem(me + step, device_total)
            pltpu.make_async_remote_copy(
                src_ref=update_buf.at[position, peer],
                dst_ref=recv_buf.at[me, position],
                send_sem=update_send,
                recv_sem=update_recv.at[position],
                device_id=(lax.rem(peer, row_count), peer // row_count),
                device_id_type=MESH,
            ).start()

        loop(1, device_total, to_peer)
        total = 2.0 * carried_buf[position] + update.astype(jnp.float32)
        for lane, lanes in enumerate(lane_blocks):
            turned[lane, pl.ds(position, length, stride=own), :] = total[:, lanes]

    loop(0, own, attend_row)

    my_columns = pl.ds(pl.multiple_of(row_id * own, own), own)
    totals = turned.reshape(len(lane_blocks), device_total, own, own, LANES)

    def summed(other, position, lane):
        devices = pl.ds(other * col_count, col_count)
        return (
            totals[lane, devices, position]
            + recv_buf[devices, position, :, lane_blocks[lane]].astype(jnp.float32)
        ).astype(jnp.bfloat16)

    def sum_remote(position):
        return pltpu.make_async_remote_copy(
            src_ref=sum_buf.at[:, position],
            dst_ref=out_ref.at[:, position, my_columns],
            send_sem=sum_send.at[position],
            recv_sem=sum_recv.at[position],
            device_id=(other_row, col_id),
            device_id_type=MESH,
        )

    def finish_position(position):
        await_bytes(recv_buf.at[pl.ds(0, device_total - 1), position], update_recv.at[position])
        for lane, lanes in enumerate(lane_blocks):
            sum_buf[:, position, :, lanes] = summed(other_row, position, lane)
        sum_remote(position).start()
        for lane, lanes in enumerate(lane_blocks):
            out_ref[:, position, my_columns, lanes] = summed(row_id, position, lane)

    loop(0, own, finish_position)

    await_bytes(recv_buf.at[pl.ds(0, device_total - 1)], update_send)
    await_bytes(
        recv_buf.at[pl.ds(0, chip_total - 1), pl.ds(0, own)], bias_send
    )

    await_bytes(row_buf.at[:, pl.ds(0, length - tile_cols)], row_send)

    def close_part(part):
        relay_copy(part).wait_send()
        col_remote(part).wait_send()
        to_pair(part).wait_send()

    loop(0, parts, close_part)

    def close_position(position):
        await_bytes(sum_buf.at[:, position], sum_recv.at[position])
        sum_remote(position).wait_send()

    loop(0, own, close_position)


def owned_columns(
    pair_state,
    residue_mask,
    chain_ids,
    gain_transition,
    hidden_weight,
    out_weight,
    gain_attention,
    query_weight,
    key_weight,
    value_weight,
    gate_weight,
    bias_weight,
    chain_weight,
    output_weight,
):
    tile_rows, tile_cols, channels = pair_state.shape
    row_count, col_count = lax.axis_size("row"), lax.axis_size("col")
    device_total = row_count * col_count
    head_count = chain_weight.shape[0]
    inner_total = key_weight.shape[1]
    length = tile_rows * row_count
    own = tile_cols // row_count
    span = col_count // row_count
    parts = PARTS
    rows_in_part = own // parts
    in_vmem = pl.BlockSpec(memory_space=pltpu.VMEM)
    in_smem = pl.BlockSpec(memory_space=pltpu.SMEM)
    dma = pltpu.SemaphoreType.DMA

    def half(*shape):
        return pltpu.VMEM(shape, jnp.bfloat16)

    def full(*shape):
        return pltpu.VMEM(shape, jnp.float32)

    out = pl.pallas_call(
        functools.partial(layer_kernel, row_count, col_count),
        out_shape=jax.ShapeDtypeStruct((col_count, own, tile_cols, channels), jnp.bfloat16),
        in_specs=[in_vmem] * 13 + [in_smem, in_vmem],
        out_specs=in_vmem,
        scratch_shapes=[
            half(own, length, channels),
            half(own, length, channels),
            half(parts, span, rows_in_part, tile_cols, channels),
            half(col_count // 2, 2, row_count, parts, rows_in_part, head_count, length),
            full(length, length),
            full(length, length),
            full(head_count, length, length),
            full(own, length, channels),
            half(own, length, channels),
            half(own, length, inner_total),
            half(own, inner_total, length),
            half(own, inner_total, length),
            full(own, inner_total, length),
            half(*query_weight.shape[::-1]),
            half(*value_weight.shape[::-1]),
            half(*gate_weight.shape[::-1]),
            full(head_count, length, length),
            half(head_count, length, length),
            half(own, device_total, own, channels),
            half(device_total, own, own, channels),
            full(channels // LANES, length * own, LANES),
            half(col_count, own, own, channels),
            dma((parts,)),
            dma((parts,)),
            dma,
            dma((parts,)),
            dma((parts,)),
            dma((parts,)),
            dma,
            dma((parts,)),
            dma((parts,)),
            dma((parts,)),
            dma,
            dma((own,)),
            dma((own,)),
            dma((own,)),
        ],
        compiler_params=pltpu.CompilerParams(
            collective_id=0, has_side_effects=True, vmem_limit_bytes=VMEM_LIMIT
        ),
        name="layer",
    )(
        pair_state.reshape(span, row_count, own, tile_cols, channels),
        jnp.transpose(pair_state, (1, 0, 2)),
        residue_mask[None, :],
        chain_ids[None, :],
        gain_transition[None, :],
        hidden_weight,
        out_weight,
        gain_attention[None, :],
        query_weight,
        key_weight,
        value_weight,
        gate_weight,
        bias_weight.T,
        chain_weight,
        output_weight,
    )
    return out.reshape(tile_rows, tile_cols, channels)


def per_device(pair_state, *others):
    tile_cols = pair_state.shape[1]
    row_count, col_count = lax.axis_size("row"), lax.axis_size("col")
    own = tile_cols // row_count
    length = row_count * pair_state.shape[0]
    fits = own == 8 and row_count == 2 and col_count % 2 == 0
    fits = fits and length == pair_state.shape[2] and length % LANES == 0
    if fits and others[11].shape[0] == own and pair_state.shape[0] == col_count * own:
        return owned_columns(pair_state, *others)
    return tile_layout(pair_state, *others)


def solution(mesh):
    placed = (
        P("row", "col", None),
        P(),
        P(),
        P(),
        P(),
        P(),
        P(),
        P(),
        P(),
        P(),
        P(),
        P(),
        P(),
        P(),
    )
    return jax.shard_map(
        per_device, mesh=mesh, in_specs=placed, out_specs=P("row", "col", None), check_vma=False
    )
```

time: 109 us -> 93.1 us (0.85)
  Pallas kernels: 99.7 us -> 88.1 us
  other arithmetic: 4.43 us -> 0 us
    pallas_call x2 -> x1, Pallas kernels: 99.7 us -> 88.1 us  [owned_columns(): pl.pallas_call(functools.partial(layer_kernel, row_count, col_count), out...]
    mul x2 -> x0, other arithmetic: 3.58 us -> none  [the longest x1 2.9 us: owned_columns(): (jnp.transpose(bias_rows, (1, 0, 2)).astype(jnp.float32) + chain_weight[:...]
    transpose x1 -> x0, local copies, waits for them, and re-layouts: 2.28 us -> none  [owned_columns(): jnp.transpose(pieces, (1, 0, 2, 3)).reshape(tile_rows, tile_cols, channels)]
    unnamed x3 -> x2, local copies, waits for them, and re-layouts: 2.54 us -> 4.79 us
where the time goes in v1:
time: 93.1 us; the launch traced here: 92.9 us
  Pallas kernels  88.1 us (95%)
  local copies, waits for them, and re-layouts  4.79 us (5%)
    pallas_call x1, Pallas kernels, owned_columns(): pl.pallas_call(functools.partial(layer_kernel, row_count, col_count), out...  88.1 us
    unnamed x2, local copies, waits for them, and re-layouts  4.79 us

profile of v1, /device:TPU:0, one launch (start us, length us, event | category | flops | bytes accessed | tf_op | source)
XLA Modules:
  0.0 92.9 jit_solution(505569360102000582)
XLA Ops:
  0.0 2.5 %copy.17 = bf16[128,16,256]{2,0,1:T(8,128)(2,1)} copy(bf16[128,16,256]{2,1,0:T(8,128)(2,1)} %param.14) | data formatting | bytes 2097152 | tf_op args[0]
  2.5 88.1 %layer.1 = bf16[16,8,16,256]{3,2,1,0:T(8,128)(2,1)} custom-call(bf16[8,2,8,16,256]{4,3,2,1,0:T(8,128)(2,1)} %bitcast.10, bf16[16,128,256]{2,1,0:T(8,128)(2,1)} %bitcast.12, s32[1,256]{1,0:T(1,128)} %bitcast.14, s32[1,256]{1,0:T(1,128)} %bitcast.15, f32[1,256]{1,0:T(1,128)} %bitcast.16, bf16[256,1024]{1,0:T(8,128)(2,1)} %hidden_weight_ref.1, ...), custom_call_target="tpu_custom_call" | custom-call | tf_op jit(solution)/shard_map/layer/pallas_call | solution.py:623
  90.7 2.3 %copy.19 = bf16[128,16,256]{2,1,0:T(8,128)(2,1)} copy(bf16[128,16,256]{2,1,0:T(8,128)(2,1)} %bitcast.11) | data formatting | bytes 2097152

commit v2 on v1

--- a/solution.py
+++ b/solution.py
@@ -11,7 +11,7 @@
 MESH = pl.DeviceIdType.MESH
 VMEM_LIMIT = 60 * 1024 * 1024
 LOG2_E = math.log2(math.e)
-PARTS = 4
+PARTS = 8
 LANES = 128
 
 mask_penalty = 1000000000.0
@@ -206,23 +206,31 @@
     row_count,
     col_count,
     tile_ref,
-    turned_ref,
     mask_ref,
     chain_ref,
     gain_transition_ref,
+    hidden_weight_hbm,
+    out_weight_hbm,
+    gain_attention_ref,
+    query_weight_hbm,
+    key_weight_hbm,
+    value_weight_hbm,
+    gate_weight_hbm,
+    bias_weight_ref,
+    chain_weight_ref,
+    output_weight_hbm,
+    out_ref,
+    tile_buf,
     hidden_weight_ref,
     out_weight_ref,
-    gain_attention_ref,
     query_weight_ref,
     key_weight_ref,
     value_weight_ref,
     gate_weight_ref,
-    bias_weight_ref,
-    chain_weight_ref,
     output_weight_ref,
-    out_ref,
     row_buf,
     col_buf,
+    turned_ref,
     relay_buf,
     bias_buf,
     same_buf,
@@ -243,14 +251,19 @@
     recv_buf,
     turned,
     sum_buf,
+    load_done,
     relay_send,
     relay_recv,
     row_send,
     row_recv,
     col_send,
     col_recv,
-    bias_send,
-    bias_recv,
+    quad_send,
+    quad_recv,
+    fan_send,
+    fan_recv,
+    last_send,
+    last_recv,
     pair_send,
     pair_recv,
     update_send,
@@ -274,6 +287,10 @@
     side = lax.rem(col_id, 2)
     pair = col_id // 2
     chip = pair * row_count + row_id
+    quarters = col_count // 4
+    far, quarter = pair // quarters, lax.rem(pair, quarters)
+    opposite_col = lax.rem(col_id + span, col_count)
+    last = parts - 1
     lane_blocks = [slice(start, start + LANES) for start in range(0, channels, LANES)]
 
     def loop(first, last, body):
@@ -335,7 +352,7 @@
 
     def col_remote(part):
         return pltpu.make_async_remote_copy(
-            src_ref=turned_ref.at[pl.ds(other_row * own + part * rows_in_part, rows_in_part)],
+            src_ref=turned_ref.at[rows_of(part)],
             dst_ref=col_buf.at[rows_of(part), own_columns, :],
             send_sem=col_send.at[part],
             recv_sem=col_recv.at[part],
@@ -343,26 +360,49 @@
             device_id_type=MESH,
         )
 
-    def own_col(part):
-        return pltpu.make_async_copy(
-            turned_ref.at[pl.ds(row_id * own + part * rows_in_part, rows_in_part)],
-            col_buf.at[rows_of(part), own_columns, :],
-            col_recv.at[part],
-        )
-
+    loads = [
+        pltpu.make_async_copy(source, target, load_done.at[index])
+        for index, (source, target) in enumerate(
+            (
+                (tile_ref, tile_buf),
+                (hidden_weight_hbm, hidden_weight_ref),
+                (out_weight_hbm, out_weight_ref),
+                (query_weight_hbm, query_weight_ref),
+                (key_weight_hbm, key_weight_ref),
+                (value_weight_hbm, value_weight_ref),
+                (gate_weight_hbm, gate_weight_ref),
+                (output_weight_hbm, output_weight_ref),
+            )
+        )
+    ]
+    loads[0].start()
     greet_all(row_count, col_count)
 
     ahead = min(2, parts)
-    for part in range(ahead):
+    for part in range(parts):
         relay_copy(part).start()
     for part in range(ahead):
         direct(part)
+    loads[0].wait()
+    for load in loads[1:]:
+        load.start()
+    tile_flat = tile_buf.reshape(tile_rows * tile_cols, channels)
+    for lane, lanes in enumerate(lane_blocks):
+        turned[lane] = tile_flat[:, lanes].astype(jnp.float32)
+
+    def turned_column(column, lane):
+        return turned[lane, pl.ds(column, tile_rows, stride=tile_cols), :].astype(jnp.bfloat16)
+
+    for position in range(own):
+        for lane, lanes in enumerate(lane_blocks):
+            turned_ref[position, :, lanes] = turned_column(other_row * own + position, lane)
     for part in range(parts):
         col_remote(part).start()
-        if part + ahead < parts:
-            relay_copy(part + ahead).start()
-        own_col(part).start()
-
+    for position in range(own):
+        for lane, lanes in enumerate(lane_blocks):
+            col_buf[position, own_columns, lanes] = turned_column(row_id * own + position, lane)
+    for load in loads[1:]:
+        load.wait()
     query_turned[...] = query_weight_ref[...].T
     value_turned[...] = value_weight_ref[...].T
     gate_turned[...] = gate_weight_ref[...].T
@@ -371,22 +411,56 @@
     penalty_row = mask_penalty * (1 - mask_ref[...]).astype(jnp.float32)
     penalty_buf[...] = jnp.broadcast_to(penalty_row, (length, length)).T
 
-    for part in range(ahead):
+    for part in range(parts):
         pass_on(part)
         if part + ahead < parts:
             direct(part + ahead)
 
     def bias_piece(part):
-        return bias_buf.at[pair, side, row_id, part]
-
-    def send_bias(part):
+        return bias_buf.at[far, quarter, side, row_id, part]
+
+    def quad_copy(part, device):
+        return pltpu.make_async_remote_copy(
+            src_ref=bias_piece(part),
+            dst_ref=bias_piece(part),
+            send_sem=quad_send,
+            recv_sem=quad_recv.at[part],
+            device_id=device,
+            device_id_type=MESH,
+        )
+
+    def send_quad(part):
+        quad_copy(part, (row_id, opposite_col)).start()
+        quad_copy(part, (other_row, opposite_col)).start()
+        quad_copy(part, (other_row, col_id)).start()
+
+    def pieces(count, rows):
+        return recv_buf.at[pl.ds(0, count), pl.ds(0, rows)]
+
+    def send_fan(part):
+        await_bytes(pieces(3, rows_in_part), quad_recv.at[part])
+
+        def to_quarter(step):
+            target = lax.rem(quarter + step, quarters)
+            pltpu.make_async_remote_copy(
+                src_ref=bias_buf.at[:, quarter, side, :, part],
+                dst_ref=bias_buf.at[:, quarter, side, :, part],
+                send_sem=fan_send,
+                recv_sem=fan_recv.at[part],
+                device_id=(row_id, (far * quarters + target) * 2 + side),
+                device_id_type=MESH,
+            ).start()
+
+        loop(1, quarters, to_quarter)
+
+    def send_last():
         def to_chip(step):
             other = lax.rem(chip + step, chip_total)
             pltpu.make_async_remote_copy(
-                src_ref=bias_piece(part),
-                dst_ref=bias_piece(part),
-                send_sem=bias_send,
-                recv_sem=bias_recv.at[part],
+                src_ref=bias_piece(last),
+                dst_ref=bias_piece(last),
+                send_sem=last_send,
+                recv_sem=last_recv,
                 device_id=(lax.rem(other, row_count), (other // row_count) * 2 + side),
                 device_id_type=MESH,
             ).start()
@@ -395,8 +469,8 @@
 
     def to_pair(part):
         return pltpu.make_async_remote_copy(
-            src_ref=bias_buf.at[:, side, :, part],
-            dst_ref=bias_buf.at[:, side, :, part],
+            src_ref=bias_buf.at[:, :, side, :, part],
+            dst_ref=bias_buf.at[:, :, side, :, part],
             send_sem=pair_send.at[part],
             recv_sem=pair_recv.at[part],
             device_id=(row_id, col_id + 1 - 2 * side),
@@ -404,7 +478,7 @@
         )
 
     def hand_over(part):
-        await_bytes(recv_buf.at[pl.ds(0, chip_total - 1), pl.ds(0, rows_in_part)], bias_recv.at[part])
+        await_bytes(pieces(4 * (quarters - 1), rows_in_part), fan_recv.at[part])
         to_pair(part).start()
 
     def transition_row(position):
@@ -420,7 +494,7 @@
         normed = normalize(carried, gain_attention_ref[...]).astype(jnp.bfloat16)
         normed_buf[position] = normed
         part = position // rows_in_part
-        bias_buf[pair, side, row_id, part, position - part * rows_in_part] = lax.dot_general(
+        bias_buf[far, quarter, side, row_id, part, position - part * rows_in_part] = lax.dot_general(
             bias_weight_ref[...],
             normed,
             (((1,), (1,)), ((), ())),
@@ -441,25 +515,28 @@
         value_buf[position] = project(value_turned).astype(jnp.bfloat16)
         gate_buf[position] = jax.nn.sigmoid(project(gate_turned))
 
+    def await_part(part):
+        await_bytes(row_buf.at[rows_of(part)], row_recv.at[part])
+        await_bytes(turned_ref.at[rows_of(part)], col_recv.at[part])
+
     def one_part(part):
-        await_bytes(row_buf.at[rows_of(part)], row_recv.at[part])
-        await_bytes(col_buf.at[rows_of(part)], col_recv.at[part])
+        await_part(part)
         loop(part * rows_in_part, (part + 1) * rows_in_part, transition_row)
-        send_bias(part)
-
-        @pl.when(part + ahead < parts)
-        def _():
-            pass_on(part + ahead)
-
-        loop(part * rows_in_part, (part + 1) * rows_in_part, project_row)
-
-        @pl.when(part > 0)
-        def _():
-            hand_over(part - 1)
-
-    loop(0, parts, one_part)
-    hand_over(parts - 1)
-    loop(0, parts, lambda part: await_bytes(bias_buf.at[:, side, :, part], pair_recv.at[part]))
+        send_quad(part)
+
+    loop(0, last, one_part)
+    await_part(last)
+    loop(0, last - 1, send_fan)
+    loop(last * rows_in_part, own, transition_row)
+    send_last()
+    send_fan(last - 1)
+    loop(0, own // 2, project_row)
+    loop(0, last - 1, hand_over)
+    loop(own // 2, own, project_row)
+    hand_over(last - 1)
+    await_bytes(pieces(chip_total - 1, rows_in_part), last_recv)
+    to_pair(last).start()
+    loop(0, parts, lambda part: await_bytes(bias_buf.at[:, :, side, :, part], pair_recv.at[part]))
 
     bias_rows = bias_buf.reshape(length * head_count, length)
     for lane, lanes in enumerate(lane_blocks):
@@ -564,10 +641,9 @@
     loop(0, own, finish_position)
 
     await_bytes(recv_buf.at[pl.ds(0, device_total - 1)], update_send)
-    await_bytes(
-        recv_buf.at[pl.ds(0, chip_total - 1), pl.ds(0, own)], bias_send
-    )
-
+    await_bytes(pieces(3, last * rows_in_part), quad_send)
+    await_bytes(pieces(4 * (quarters - 1), last * rows_in_part), fan_send)
+    await_bytes(pieces(chip_total - 1, rows_in_part), last_send)
     await_bytes(row_buf.at[:, pl.ds(0, length - tile_cols)], row_send)
 
     def close_part(part):
@@ -611,6 +687,7 @@
     parts = PARTS
     rows_in_part = own // parts
     in_vmem = pl.BlockSpec(memory_space=pltpu.VMEM)
+    in_hbm = pl.BlockSpec(memory_space=pl.ANY)
     in_smem = pl.BlockSpec(memory_space=pltpu.SMEM)
     dma = pltpu.SemaphoreType.DMA
 
@@ -623,13 +700,37 @@
     out = pl.pallas_call(
         functools.partial(layer_kernel, row_count, col_count),
         out_shape=jax.ShapeDtypeStruct((col_count, own, tile_cols, channels), jnp.bfloat16),
-        in_specs=[in_vmem] * 13 + [in_smem, in_vmem],
+        in_specs=[
+            in_hbm,
+            in_vmem,
+            in_vmem,
+            in_vmem,
+            in_hbm,
+            in_hbm,
+            in_vmem,
+            in_hbm,
+            in_hbm,
+            in_hbm,
+            in_hbm,
+            in_vmem,
+            in_smem,
+            in_hbm,
+        ],
         out_specs=in_vmem,
         scratch_shapes=[
+            half(span, row_count, own, tile_cols, channels),
+            half(*hidden_weight.shape),
+            half(*out_weight.shape),
+            half(*query_weight.shape),
+            half(*key_weight.shape),
+            half(*value_weight.shape),
+            half(*gate_weight.shape),
+            half(*output_weight.shape),
             half(own, length, channels),
             half(own, length, channels),
+            half(own, tile_rows, channels),
             half(parts, span, rows_in_part, tile_cols, channels),
-            half(col_count // 2, 2, row_count, parts, rows_in_part, head_count, length),
+            half(2, col_count // 4, 2, row_count, parts, rows_in_part, head_count, length),
             full(length, length),
             full(length, length),
             full(head_count, length, length),
@@ -648,6 +749,7 @@
             half(device_total, own, own, channels),
             full(channels // LANES, length * own, LANES),
             half(col_count, own, own, channels),
+            dma((8,)),
             dma((parts,)),
             dma((parts,)),
             dma,
@@ -656,6 +758,10 @@
             dma((parts,)),
             dma,
             dma((parts,)),
+            dma,
+            dma((parts,)),
+            dma,
+            dma,
             dma((parts,)),
             dma((parts,)),
             dma,
@@ -669,7 +775,6 @@
         name="layer",
     )(
         pair_state.reshape(span, row_count, own, tile_cols, channels),
-        jnp.transpose(pair_state, (1, 0, 2)),
         residue_mask[None, :],
         chain_ids[None, :],
         gain_transition[None, :],
@@ -692,7 +797,7 @@
     row_count, col_count = lax.axis_size("row"), lax.axis_size("col")
     own = tile_cols // row_count
     length = row_count * pair_state.shape[0]
-    fits = own == 8 and row_count == 2 and col_count % 2 == 0
+    fits = own == 8 and row_count == 2 and col_count % 4 == 0
     fits = fits and length == pair_state.shape[2] and length % LANES == 0
     if fits and others[11].shape[0] == own and pair_state.shape[0] == col_count * own:
         return owned_columns(pair_state, *others)

time: 93.1 us -> 84.1 us (0.903)
  Pallas kernels: 88.1 us -> 81.6 us
  local copies, waits for them, and re-layouts: 4.79 us -> 2.26 us
    pallas_call x1, Pallas kernels: 88.1 us -> 81.6 us  [owned_columns(): pl.pallas_call(functools.partial(layer_kernel, row_count, col_count), out...]
    unnamed x2 -> x1, local copies, waits for them, and re-layouts: 4.79 us -> 2.26 us
where the time goes in v2:
time: 84.1 us; the launch traced here: 83.9 us
  Pallas kernels  81.6 us (97%)
  local copies, waits for them, and re-layouts  2.26 us (3%)
    pallas_call x1, Pallas kernels, owned_columns(): pl.pallas_call(functools.partial(layer_kernel, row_count, col_count), out...  81.6 us
    unnamed x1, local copies, waits for them, and re-layouts  2.26 us

profile of v2, /device:TPU:0, one launch (start us, length us, event | category | flops | bytes accessed | tf_op | source)
XLA Modules:
  0.0 83.9 jit_solution(10762018074737219992)
XLA Ops:
  0.0 81.6 %layer.1 = bf16[16,8,16,256]{3,2,1,0:T(8,128)(2,1)} custom-call(bf16[8,2,8,16,256]{4,3,2,1,0:T(8,128)(2,1)} %bitcast.8, s32[1,256]{1,0:T(1,128)} %bitcast.10, s32[1,256]{1,0:T(1,128)} %bitcast.11, f32[1,256]{1,0:T(1,128)} %bitcast.12, bf16[256,1024]{1,0:T(8,128)(2,1)} %hidden_weight_hbm.1, bf16[1024,256]{1,0:T(8,128)(2,1)} %out_weight_hbm.1, ...), custom_call_target="tpu_custom_call" | custom-call | tf_op jit(solution)/shard_map/layer/pallas_call | solution.py:700
  81.6 2.3 %copy.16 = bf16[128,16,256]{2,1,0:T(8,128)(2,1)} copy(bf16[128,16,256]{2,1,0:T(8,128)(2,1)} %bitcast.7) | data formatting | bytes 2097152

commit v3 on v2

--- a/solution.py
+++ b/solution.py
@@ -526,14 +526,15 @@
 
     loop(0, last, one_part)
     await_part(last)
-    loop(0, last - 1, send_fan)
+    early = last * 5 // 8
+    loop(0, early, send_fan)
     loop(last * rows_in_part, own, transition_row)
     send_last()
-    send_fan(last - 1)
+    loop(early, last, send_fan)
     loop(0, own // 2, project_row)
-    loop(0, last - 1, hand_over)
+    loop(0, early, hand_over)
     loop(own // 2, own, project_row)
-    hand_over(last - 1)
+    loop(early, last, hand_over)
     await_bytes(pieces(chip_total - 1, rows_in_part), last_recv)
     to_pair(last).start()
     loop(0, parts, lambda part: await_bytes(bias_buf.at[:, :, side, :, part], pair_recv.at[part]))

time: 84.1 us -> 83.2 us (0.989)
    pallas_call x1, Pallas kernels: 81.6 us -> 80.8 us  [owned_columns(): pl.pallas_call(functools.partial(layer_kernel, row_count, col_count), out...]
where the time goes in v3:
time: 83.2 us; the launch traced here: 83 us
  Pallas kernels  80.8 us (97%)
  local copies, waits for them, and re-layouts  2.26 us (3%)
    pallas_call x1, Pallas kernels, owned_columns(): pl.pallas_call(functools.partial(layer_kernel, row_count, col_count), out...  80.8 us
    unnamed x1, local copies, waits for them, and re-layouts  2.26 us

profile of v3, /device:TPU:0, one launch (start us, length us, event | category | flops | bytes accessed | tf_op | source)
XLA Modules:
  0.0 83.0 jit_solution(13608187320258160954)
XLA Ops:
  0.0 80.8 %layer.1 = bf16[16,8,16,256]{3,2,1,0:T(8,128)(2,1)} custom-call(bf16[8,2,8,16,256]{4,3,2,1,0:T(8,128)(2,1)} %bitcast.8, s32[1,256]{1,0:T(1,128)} %bitcast.10, s32[1,256]{1,0:T(1,128)} %bitcast.11, f32[1,256]{1,0:T(1,128)} %bitcast.12, bf16[256,1024]{1,0:T(8,128)(2,1)} %hidden_weight_hbm.1, bf16[1024,256]{1,0:T(8,128)(2,1)} %out_weight_hbm.1, ...), custom_call_target="tpu_custom_call" | custom-call | tf_op jit(solution)/shard_map/layer/pallas_call | solution.py:701
  80.8 2.3 %copy.16 = bf16[128,16,256]{2,1,0:T(8,128)(2,1)} copy(bf16[128,16,256]{2,1,0:T(8,128)(2,1)} %bitcast.7) | data formatting | bytes 2097152
